TPU v7x, 32 devices: a whole 2x2x4 slice. The times are simulated.
32 devices in a mesh: dp: 8 (over z, y), ctx: 4 (over x, core).
Axes of the slice: x: 2, y: 2, z: 4, core: 2. Of those that a mesh axis runs over, the one named last changes fastest.
Arguments:
- tokens: bfloat16 [8, 1024, 1024], P('dp', 'ctx'), may hold values from -6 to 6
- doc_ids: int32 [8, 1024], P('dp', 'ctx'), may hold values from 0 to 7, never falling along the last dimension, each value on 1 to 512 neighbouring positions
- w_query: bfloat16 [1024, 1024], P(('dp', 'ctx')), may hold values from -0.1875 to 0.1875
- key_weight: bfloat16 [1024, 512], P(('dp', 'ctx')), may hold values from -0.1875 to 0.1875
- value_weight: bfloat16 [1024, 512], P(('dp', 'ctx')), may hold values from -0.1875 to 0.1875
- w_output: bfloat16 [1024, 1024], P(None, ('dp', 'ctx')), may hold values from -1.5 to 1.5
- w_gate: bfloat16 [1024, 4608], P(('dp', 'ctx')), may hold values from -0.1875 to 0.1875
- w_up: bfloat16 [1024, 4608], P(('dp', 'ctx')), may hold values from -0.1875 to 0.1875
- w_down: bfloat16 [4608, 1024], P(None, ('dp', 'ctx')), may hold values from -0.09375 to 0.09375
- norm_gains: bfloat16 [2, 1024], P(None, ('dp', 'ctx')), may hold values from 0.5 to 1.5
- head_norm_gains: bfloat16 [2, 64], replicated, may hold values from 0.5 to 1.5
- out_grad: bfloat16 [8, 1024, 1024], P('dp', 'ctx'), may hold values from -6 to 6
Outputs:
- layer_out: bfloat16 [8, 1024, 1024], P('dp', 'ctx')
- input_grad: bfloat16 [8, 1024, 1024], P('dp', 'ctx')
- grad_query: bfloat16 [1024, 1024], P(('dp', 'ctx'))
- grad_key: bfloat16 [1024, 512], P(('dp', 'ctx'))
- grad_value: bfloat16 [1024, 512], P(('dp', 'ctx'))
- grad_output: bfloat16 [1024, 1024], P(None, ('dp', 'ctx'))
- grad_gate: bfloat16 [1024, 4608], P(('dp', 'ctx'))
- grad_up: bfloat16 [1024, 4608], P(('dp', 'ctx'))
- grad_down: bfloat16 [4608, 1024], P(None, ('dp', 'ctx'))
- grad_norms: bfloat16 [2, 1024], P(None, ('dp', 'ctx'))
- grad_heads: bfloat16 [2, 64], replicated
Inputs may be any that keep to these rules, and one draw needn't show every extreme that they name: `doc_ids`: along each sequence the numbers never fall; each document spans 1 to 512 tokens.
All inputs are finite; a program needn't handle non-finite values.
Results may differ from a plain program's by a relative error of at most 0.015.
Values may be sent and summed in bfloat16 or wider, within the bound.
No kernel may reach another device: no remote copies, remote signals or barrier semaphores. Data moves between devices by JAX's collectives and lax.ppermute only.
A program may use at most 320 MiB of HBM per device.

v0:
```python
import math
import jax
import jax.numpy as jnp
from jax import lax
from jax.sharding import PartitionSpec as P

EPS = 1e-05
THETA = 1000000.0
BF = jnp.bfloat16
F32 = jnp.float32
ALL = ("dp", "ctx")


def add_low(a, b):
    return (a.astype(F32) + b.astype(F32)).astype(BF)


def flip(value, axis, size, bits):
    return lax.ppermute(value, axis, [(i, i ^ bits) for i in range(size)])


def gather_ctx(own):
    core = flip(own, "ctx", 4, 1)
    across = flip(own, "ctx", 4, 2)
    return [own, core, across, flip(across, "ctx", 4, 1)]


def scatter_ctx(parts):
    far = flip(parts[3], "ctx", 4, 1)
    near = flip(parts[1], "ctx", 4, 1)
    far_sum = add_low(parts[2], far)
    far_in = flip(far_sum, "ctx", 4, 2)
    return parts[0].astype(F32) + near.astype(F32) + far_in.astype(F32)


def exchange_ctx(parts):
    return [parts[0]] + [flip(parts[j], "ctx", 4, j) for j in range(1, 4)]


def place(parts, where, axis):
    size = parts[0].shape[axis]
    shape = list(parts[0].shape)
    shape[axis] = size * len(parts)
    out = jnp.zeros(shape, parts[0].dtype)
    for part, at in zip(parts, where):
        out = lax.dynamic_update_slice_in_dim(out, part, at * size, axis)
    return out


def ring(value, size):
    return lax.ppermute(value, "dp", [(i, (i + 2) % size) for i in range(size)])


def gather_dp(block, size):
    if size < 4 or size > 8:
        return lax.all_gather(block, "dp", axis=0, tiled=True)
    me = lax.axis_index("dp")
    parts, where = ([], [])
    for step in range(size // 2):
        at = (me - 2 * step) % size
        parts += [block, flip(block, "dp", size, 1)]
        where += [at, at ^ 1]
        if step + 1 < size // 2:
            block = ring(block, size)
    return place(parts, where, 0)


def scatter_dp(whole, size):
    if size < 4 or size > 8:
        return lax.psum_scatter(whole, "dp", scatter_dimension=0, tiled=True).astype(F32)
    me = lax.axis_index("dp")
    rows = whole.shape[0] // size

    def part(at):
        return lax.dynamic_slice_in_dim(whole, at * rows, rows, 0)

    total = None
    for step in range(size // 2):
        at = (me - 2 * (step + 1)) % size
        near = flip(part(at ^ 1), "dp", size, 1)
        own = part(at).astype(F32) + near.astype(F32)
        if total is not None:
            own = own + ring(total, size).astype(F32)
        total = own.astype(BF)
    return own


def sum_all(value, dp_size):
    for bits in (1, 2):
        value = value + flip(value, "ctx", 4, bits)
    bits = 1
    while bits < dp_size:
        value = value + flip(value, "dp", dp_size, bits)
        bits *= 2
    return value


def dot(a, b):
    return lax.dot_general(a, b, (((1,), (0,)), ((), ())), preferred_element_type=F32)


def dot_nt(a, b):
    return lax.dot_general(a, b, (((1,), (1,)), ((), ())), preferred_element_type=F32)


def dot_tn(a, b):
    return lax.dot_general(a, b, (((0,), (0,)), ((), ())), preferred_element_type=F32)


def rms_scale(values, gain_row):
    return values * lax.rsqrt(jnp.mean(values * values, -1, keepdims=True) + EPS) * gain_row


def rope_tables(positions, width_all):
    half_width = width_all // 2
    freqs = THETA ** (-(2.0 * jnp.arange(half_width, dtype=jnp.float32)) / width_all)
    angles = positions.astype(jnp.float32)[..., None] * freqs
    angles = jnp.concatenate([angles, angles], -1)
    return (jnp.cos(angles), jnp.sin(angles))


def rotate(values, cosine_table, sine_table):
    half_width = values.shape[-1] // 2
    turned = jnp.concatenate([-values[..., half_width:], values[..., :half_width]], -1)
    return values * cosine_table + turned * sine_table


def head_prepare(projected, gain_row, cosine_table, sine_table, head_count):
    shaped = projected.reshape(projected.shape[:-1] + (head_count, gain_row.shape[0]))
    normed = rms_scale(shaped, gain_row)
    return rotate(normed, cosine_table[..., None, :], sine_table[..., None, :])


def split_parts(tall, count):
    rows = tall.shape[0] // count
    return [lax.slice_in_dim(tall, j * rows, (j + 1) * rows, axis=0) for j in range(count)]


def on_device(
    dp_size,
    tokens,
    doc_ids,
    w_query,
    key_weight,
    value_weight,
    w_output,
    w_gate,
    w_up,
    w_down,
    norm_gains,
    head_norm_gains,
    out_grad,
):
    local_len, model_dim = tokens.shape[1:]
    tokens, out_grad, doc_row = (tokens[0], out_grad[0], doc_ids[0])
    head_dim = head_norm_gains.shape[1]
    q_cols, kv_cols = (w_query.shape[1] // 4, key_weight.shape[1] // 4)
    q_heads, kv_heads = (q_cols // head_dim, kv_cols // head_dim)
    group_size = q_heads // kv_heads
    scale_by = 1.0 / math.sqrt(head_dim)
    shard = norm_gains.shape[1]
    ff_cols = w_gate.shape[1] // 4
    me = lax.axis_index("ctx")
    places = [me ^ j for j in range(4)]

    def spread(pieces):
        sent = []
        for at in places:
            cut = [
                lax.dynamic_slice_in_dim(p, at * (p.shape[1] // 4), p.shape[1] // 4, 1)
                for p in pieces
            ]
            sent.append(jnp.concatenate(cut, 1))
        block = place(exchange_ctx(sent), places, 0)
        return gather_dp(block, dp_size)

    gains_full = lax.all_gather(norm_gains, ALL, axis=1, tiled=True).astype(F32)
    attn_w = spread([w_query, key_weight, value_weight, w_output.T])
    wq = attn_w[:, :q_cols]
    wk = attn_w[:, q_cols : q_cols + kv_cols]
    wv = attn_w[:, q_cols + kv_cols : q_cols + 2 * kv_cols]
    wo_t = attn_w[:, q_cols + 2 * kv_cols :]
    wg = spread([w_gate])
    wu = spread([w_up])
    wd_t = spread([w_down.T])
    head_full = head_norm_gains.astype(F32)
    docs = jnp.concatenate(gather_ctx(doc_row.reshape(1, -1)), 1)[0]
    all_tokens = jnp.concatenate(gather_ctx(tokens), 0)
    all_grad = jnp.concatenate(gather_ctx(out_grad), 0)
    index = jnp.concatenate(
        [at * local_len + jnp.arange(local_len, dtype=jnp.int32) for at in places]
    )
    earlier = jnp.sum((docs[None, :] < docs[:, None]).astype(jnp.int32), -1)
    positions = index - earlier
    visible = (docs[None, :] == docs[:, None]) & (index[None, :] <= index[:, None])
    cosine_table, sine_table = rope_tables(positions, head_dim)
    inputs = all_tokens.astype(F32)
    normed_one = rms_scale(inputs, gains_full[0]).astype(BF)
    q_pre = dot(normed_one, wq)
    k_pre = dot(normed_one, wk)
    value_rows = dot(normed_one, wv).astype(BF)
    query_rows = head_prepare(q_pre, head_full[0], cosine_table, sine_table, q_heads).astype(BF)
    key_rows = head_prepare(k_pre, head_full[1], cosine_table, sine_table, kv_heads).astype(BF)
    value_rows = value_rows.reshape(-1, kv_heads, head_dim)
    grouped = query_rows.reshape(-1, kv_heads, group_size, head_dim)

    def attend_scores():
        raw = jnp.einsum("tkgd,skd->kgts", grouped, key_rows, preferred_element_type=F32) * scale_by
        return jnp.where(visible[None, None], raw, -1e30)

    scores = attend_scores()
    top_row = jnp.max(scores, -1, keepdims=True)
    expd = jnp.exp(scores - top_row)
    total_row = jnp.sum(expd, -1, keepdims=True)
    probs = expd / total_row
    log_total = top_row + jnp.log(total_row)
    mixed = jnp.einsum("kgts,skd->tkgd", probs.astype(BF), value_rows, preferred_element_type=F32)
    attn_out = mixed.reshape(-1, q_cols).astype(BF)
    resid_sum = scatter_ctx(split_parts(dot_nt(attn_out, wo_t).astype(BF), 4))
    resid = tokens.astype(F32) + resid_sum
    normed_own = rms_scale(resid, gains_full[1]).astype(BF)
    normed_two = jnp.concatenate(gather_ctx(normed_own), 0)
    gate_act = dot(normed_two, wg)
    up_act = dot(normed_two, wu)
    hidden = (jax.nn.silu(gate_act) * up_act).astype(BF)
    grad_hidden = dot(all_grad, wd_t)
    _, gate_pull = jax.vjp(lambda g, u: jax.nn.silu(g) * u, gate_act, up_act)
    grad_gate_full, grad_up_full = gate_pull(grad_hidden)
    grad_gate = grad_gate_full.astype(BF)
    grad_up = grad_up_full.astype(BF)
    grad_two_part = (dot_nt(grad_gate, wg) + dot_nt(grad_up, wu)).astype(BF)
    grad_norm_two = scatter_ctx(split_parts(grad_two_part, 4))
    _, second_pull = jax.vjp(rms_scale, resid, gains_full[1])
    grad_resid_norm, grad_gain_two = second_pull(grad_norm_two)
    grad_resid = out_grad.astype(F32) + grad_resid_norm
    down_part = dot_nt(hidden, wd_t).astype(BF)
    layer_out = (resid + scatter_ctx(split_parts(down_part, 4))).astype(BF)

    def collect(whole, widths):
        mine = scatter_dp(whole.astype(BF), dp_size).astype(BF)
        sent = [lax.dynamic_slice_in_dim(mine, at * shard, shard, 0) for at in places]
        got = exchange_ctx(sent)
        outs, start = ([], 0)
        for width in widths:
            cut = [g[:, start : start + width] for g in got]
            outs.append(place(cut, places, 1))
            start += width
        return outs

    (grad_g_out,) = collect(dot_tn(normed_two, grad_gate), (ff_cols,))
    (grad_u_out,) = collect(dot_tn(normed_two, grad_up), (ff_cols,))
    (grad_d_out,) = collect(dot_tn(all_grad, hidden), (ff_cols,))
    grad_attn = jnp.concatenate(gather_ctx(grad_resid.astype(BF)), 0)
    grad_mixed = dot(grad_attn, wo_t).astype(BF)
    grad_grouped = grad_mixed.reshape(-1, kv_heads, group_size, head_dim)
    probs = jnp.exp(attend_scores() - log_total)
    grad_probs = jnp.einsum("tkgd,skd->kgts", grad_grouped, value_rows, preferred_element_type=F32)
    value_part = jnp.einsum(
        "kgts,tkgd->skd", probs.astype(BF), grad_grouped, preferred_element_type=F32
    )
    inner_row = jnp.sum(probs * grad_probs, -1, keepdims=True)
    grad_scores = (probs * (grad_probs - inner_row)).astype(BF)
    grad_queries = (
        jnp.einsum("kgts,skd->tkgd", grad_scores, key_rows, preferred_element_type=F32) * scale_by
    )
    grad_keys = (
        jnp.einsum("kgts,tkgd->skd", grad_scores, grouped, preferred_element_type=F32) * scale_by
    )
    _, query_pull = jax.vjp(
        lambda v, g: head_prepare(v, g, cosine_table, sine_table, q_heads), q_pre, head_full[0]
    )
    grad_q_pre, grad_q_gain = query_pull(grad_queries.reshape(-1, q_heads, head_dim))
    _, key_pull = jax.vjp(
        lambda v, g: head_prepare(v, g, cosine_table, sine_table, kv_heads), k_pre, head_full[1]
    )
    grad_k_pre, grad_k_gain = key_pull(grad_keys)
    grad_qkv = jnp.concatenate(
        [grad_q_pre.astype(BF), grad_k_pre.astype(BF), value_part.reshape(-1, kv_cols).astype(BF)],
        1,
    )
    w_qkv = attn_w[:, : q_cols + 2 * kv_cols]
    grad_one_part = dot_nt(grad_qkv, w_qkv)
    _, first_pull = jax.vjp(rms_scale, inputs, gains_full[0])
    grad_gain_one = first_pull(grad_one_part)[1]
    grad_norm_one = scatter_ctx(split_parts(grad_one_part.astype(BF), 4))
    _, own_pull = jax.vjp(rms_scale, tokens.astype(F32), gains_full[0])
    input_grad = (grad_resid + own_pull(grad_norm_one)[0]).astype(BF)
    grad_attn_w = jnp.concatenate([dot_tn(normed_one, grad_qkv), dot_tn(grad_attn, attn_out)], 1)
    grad_q_out, grad_k_out, grad_v_out, grad_o_out = collect(
        grad_attn_w, (q_cols, kv_cols, kv_cols, q_cols)
    )
    small = jnp.concatenate([grad_gain_one, grad_gain_two, grad_q_gain, grad_k_gain])
    small = sum_all(small.reshape(1, -1), dp_size)[0]
    norm_total = small[: 2 * model_dim].reshape(2, model_dim)
    head_sum = small[2 * model_dim :].reshape(2, head_dim)
    norm_own = lax.dynamic_slice_in_dim(norm_total, lax.axis_index(ALL) * shard, shard, 1)
    return (
        layer_out[None],
        input_grad[None],
        grad_q_out,
        grad_k_out,
        grad_v_out,
        grad_o_out.T,
        grad_g_out,
        grad_u_out,
        grad_d_out.T,
        norm_own.astype(BF),
        head_sum.astype(BF),
    )


def solution(mesh):

    def step(*arrays):
        return on_device(mesh.shape["dp"], *arrays)

    in_specs = (
        P("dp", "ctx", None),
        P("dp", "ctx"),
        P(("dp", "ctx"), None),
        P(("dp", "ctx"), None),
        P(("dp", "ctx"), None),
        P(None, ("dp", "ctx")),
        P(("dp", "ctx"), None),
        P(("dp", "ctx"), None),
        P(None, ("dp", "ctx")),
        P(None, ("dp", "ctx")),
        P(),
        P("dp", "ctx", None),
    )
    out_specs = (
        P("dp", "ctx", None),
        P("dp", "ctx", None),
        P(("dp", "ctx"), None),
        P(("dp", "ctx"), None),
        P(("dp", "ctx"), None),
        P(None, ("dp", "ctx")),
        P(("dp", "ctx"), None),
        P(("dp", "ctx"), None),
        P(None, ("dp", "ctx")),
        P(None, ("dp", "ctx")),
        P(),
    )
    return jax.shard_map(step, mesh=mesh, in_specs=in_specs, out_specs=out_specs, check_vma=False)
```

profile of v0, /device:TPU:0, one launch (start us, length us, event | category | flops | bytes accessed | tf_op | source)
XLA Modules:
  0.0 532.0 jit_solution(6411378108556584978)
XLA Ops:
  10.2 41.8 %all-gather = bf16[32,32,2]{1,2,0:T(2,128)(2,1)S(1)} all-gather(bf16[1,32,2]{1,2,0:T(2,128)(2,1)} %bitcast.173), channel_id=1, replica_groups=mesh['dp'=8,'ctx'=4] {'dp','ctx'}, dimensions={0}, use_global_device_ids=true | all-gather | bytes 4224 | tf_op jit(solution)/shard_map/all_gather | solution.py:177
  96.7 8.2 %collective-permute-done.36 = bf16[128,1152]{1,0:T(8,128)(2,1)S(1)} collective-permute-done((bf16[128,1152]{1,0:T(8,128)(2,1)S(1)}, bf16[128,1152]{1,0:T(8,128)(2,1)S(1)}, u32[]{:S(2)}, u32[]{:S(2)}) %collective-permute-start.36) | collective-permute-done | bytes 294944 | tf_op jit(solution)/shard_map/ppermute | solution.py:51
  106.3 7.9 %collective-permute-done.46 = bf16[128,1152]{1,0:T(8,128)(2,1)S(1)} collective-permute-done((bf16[128,1152]{1,0:T(8,128)(2,1)S(1)}, bf16[128,1152]{1,0:T(8,128)(2,1)S(1)}, u32[]{:S(2)}, u32[]{:S(2)}) %collective-permute-start.46) | collective-permute-done | bytes 294944 | tf_op jit(solution)/shard_map/ppermute | solution.py:51
  133.3 10.3 %collective-permute-done.38 = bf16[128,1152]{1,0:T(8,128)(2,1)} collective-permute-done((bf16[128,1152]{1,0:T(8,128)(2,1)S(1)}, bf16[128,1152]{1,0:T(8,128)(2,1)}, u32[]{:S(2)}, u32[]{:S(2)}) %collective-permute-start.38) | collective-permute-done | bytes 294944 | tf_op jit(solution)/shard_map/ppermute | solution.py:51
  179.5 7.5 %fusion.97 = (f32[2,2,1024]{2,1,0:T(2,128)S(1)}, f32[2,2,1024,1024]{2,3,1,0:T(8,128)}) fusion(bf16[1024,2,64,1]{0,2,3,1:T(8,128)(2,1)S(1)} %fusion.47, bf16[1024,2,2,64]{0,3,2,1:T(8,128)(2,1)S(1)} %fusion.34, pred[1024,1024]{0,1:T(8,128)(4,1)S(1)} %copy-done.26), kind=kOutput, calls=%fused_computation.347 | convolution fusion | flops 549449728 | bytes 18628608 | tf_op jit(solution)/shard_map/tkgd,skd->kgts/dot_general | solution.py:208
  186.9 8.0 %fusion.3 = f32[2,2,1024]{2,1,0:T(2,128)S(1)} fusion(f32[2,2,1024,1024]{2,3,1,0:T(8,128)} %get-tuple-element.138, f32[2,2,1024]{2,1,0:T(2,128)S(1)} %get-tuple-element.137), kind=kLoop, calls=%fused_computation.9 | loop fusion | flops 8384512 | bytes 16809984 | tf_op jit(solution)/shard_map/reduce_sum | solution.py:214
  194.9 7.5 %fusion.18 = bf16[2,64,2,1024]{3,1,2,0:T(8,128)(2,1)S(1)} fusion(bf16[1024,2,64,1]{0,2,3,1:T(8,128)(2,1)S(1)} %bitcast.152, f32[2,2,1024,1024]{2,3,1,0:T(8,128)} %get-tuple-element.138, f32[2,2,1024]{2,1,0:T(2,128)S(1)} %fusion.3, f32[2,2,1024]{2,1,0:T(2,128)S(1)} %get-tuple-element.137), kind=kOutput, calls=%fused_computation.68 | convolution fusion | flops 549715968 | bytes 17596416 | tf_op jit(solution)/shard_map/kgts,skd->tkgd/dot_general | solution.py:217
  206.4 13.0 %collective-permute-start.50 = (bf16[128,1152]{1,0:T(8,128)(2,1)}, bf16[128,1152]{1,0:T(8,128)(2,1)S(1)}, u32[]{:S(2)}, u32[]{:S(2)}) collective-permute-start(bf16[128,1152]{1,0:T(8,128)(2,1)} %collective-permute-done.48), channel_id=1, source_target_pairs={{0,8},{4,12},{8,16},{12,20},{16,24},{20,28},{24,0},{28,4},{1,9},{5... | collective-permute-start | bytes 884744 | tf_op jit(solution)/shard_map/ppermute | solution.py:51
  221.2 9.1 %collective-permute-done.50 = bf16[128,1152]{1,0:T(8,128)(2,1)S(1)} collective-permute-done((bf16[128,1152]{1,0:T(8,128)(2,1)}, bf16[128,1152]{1,0:T(8,128)(2,1)S(1)}, u32[]{:S(2)}, u32[]{:S(2)}) %collective-permute-start.50) | collective-permute-done | bytes 294944 | tf_op jit(solution)/shard_map/ppermute | solution.py:51
  236.5 15.1 %collective-permute-done.41 = bf16[128,1152]{1,0:T(8,128)(2,1)S(1)} collective-permute-done((bf16[128,1152]{1,0:T(8,128)(2,1)}, bf16[128,1152]{1,0:T(8,128)(2,1)S(1)}, u32[]{:S(2)}, u32[]{:S(2)}) %collective-permute-start.41) | collective-permute-done | bytes 294944 | tf_op jit(solution)/shard_map/ppermute | solution.py:19
  252.9 11.4 %collective-permute-done.20 = bf16[256,1024]{1,0:T(8,128)(2,1)S(1)} collective-permute-done((bf16[256,1024]{1,0:T(8,128)(2,1)S(1)}, bf16[256,1024]{1,0:T(8,128)(2,1)S(1)}, u32[]{:S(2)}, u32[]{:S(2)}) %collective-permute-start.20) | collective-permute-done | bytes 524320 | tf_op jit(solution)/shard_map/ppermute | solution.py:19
  273.3 8.2 %fusion.13 = (bf16[1024,1152]{1,0:T(8,128)(2,1)}, bf16[1024,1152]{1,0:T(8,128)(2,1)}, bf16[1024,1152]{1,0:T(8,128)(2,1)S(1)}) fusion(f32[1024,1152]{1,0:T(8,128)S(1)} %fusion.46, f32[1024,1152]{1,0:T(8,128)S(1)} %fusion.77, bf16[1024,1152]{1,0:T(8,128)(2,1)S(1)} %constant_dynamic-update-slice_fusion.47, bf16[256,1024]{1,0:T(8,128)(2,1)S(1)} %collective-permute-done.21, ...), kind=kOutput, calls=%fused_computation.21 | convolution fusion | flops 2443182080 | bytes 20971520 | tf_op jit(solution)/shard_map/dot_general | solution.py:99
  310.4 7.9 %collective-permute-done.90 = bf16[128,1152]{1,0:T(8,128)(2,1)S(1)} collective-permute-done((bf16[128,1152]{1,0:T(8,128)(2,1)S(1)}, bf16[128,1152]{1,0:T(8,128)(2,1)S(1)}, u32[]{:S(2)}, u32[]{:S(2)}) %collective-permute-start.90) | collective-permute-done | bytes 294944 | tf_op jit(solution)/shard_map/ppermute | solution.py:19
  318.9 8.0 %collective-permute-done.80 = bf16[128,1152]{1,0:T(8,128)(2,1)S(1)} collective-permute-done((bf16[128,1152]{1,0:T(8,128)(2,1)S(1)}, bf16[128,1152]{1,0:T(8,128)(2,1)S(1)}, u32[]{:S(2)}, u32[]{:S(2)}) %collective-permute-start.80) | collective-permute-done | bytes 294944 | tf_op jit(solution)/shard_map/ppermute | solution.py:19
  329.5 8.7 %collective-permute-done.101 = bf16[128,1152]{1,0:T(8,128)(2,1)S(1)} collective-permute-done((bf16[128,1152]{1,0:T(8,128)(2,1)S(1)}, bf16[128,1152]{1,0:T(8,128)(2,1)S(1)}, u32[]{:S(2)}, u32[]{:S(2)}) %collective-permute-start.101) | collective-permute-done | bytes 294944 | tf_op jit(solution)/shard_map/ppermute | solution.py:51
  338.8 9.9 %collective-permute-done.91 = bf16[128,1152]{1,0:T(8,128)(2,1)S(1)} collective-permute-done((bf16[128,1152]{1,0:T(8,128)(2,1)S(1)}, bf16[128,1152]{1,0:T(8,128)(2,1)S(1)}, u32[]{:S(2)}, u32[]{:S(2)}) %collective-permute-start.91) | collective-permute-done | bytes 294944 | tf_op jit(solution)/shard_map/ppermute | solution.py:51
  349.2 9.1 %collective-permute-done.81 = bf16[128,1152]{1,0:T(8,128)(2,1)S(1)} collective-permute-done((bf16[128,1152]{1,0:T(8,128)(2,1)S(1)}, bf16[128,1152]{1,0:T(8,128)(2,1)S(1)}, u32[]{:S(2)}, u32[]{:S(2)}) %collective-permute-start.81) | collective-permute-done | bytes 294944 | tf_op jit(solution)/shard_map/ppermute | solution.py:51
  358.8 8.1 %collective-permute-done.102 = bf16[128,1152]{1,0:T(8,128)(2,1)S(1)} collective-permute-done((bf16[128,1152]{1,0:T(8,128)(2,1)S(1)}, bf16[128,1152]{1,0:T(8,128)(2,1)S(1)}, u32[]{:S(2)}, u32[]{:S(2)}) %collective-permute-start.102) | collective-permute-done | bytes 294944 | tf_op jit(solution)/shard_map/ppermute | solution.py:51
  367.4 8.0 %collective-permute-done.92 = bf16[128,1152]{1,0:T(8,128)(2,1)S(1)} collective-permute-done((bf16[128,1152]{1,0:T(8,128)(2,1)S(1)}, bf16[128,1152]{1,0:T(8,128)(2,1)S(1)}, u32[]{:S(2)}, u32[]{:S(2)}) %collective-permute-start.92) | collective-permute-done | bytes 294944 | tf_op jit(solution)/shard_map/ppermute | solution.py:51
  375.9 8.0 %collective-permute-done.82 = bf16[128,1152]{1,0:T(8,128)(2,1)S(1)} collective-permute-done((bf16[128,1152]{1,0:T(8,128)(2,1)S(1)}, bf16[128,1152]{1,0:T(8,128)(2,1)S(1)}, u32[]{:S(2)}, u32[]{:S(2)}) %collective-permute-start.82) | collective-permute-done | bytes 294944 | tf_op jit(solution)/shard_map/ppermute | solution.py:51
  428.2 8.5 %fusion = (f32[2,2,1024]{2,1,0:T(2,128)S(1)}, f32[2,1024,1024,2]{2,1,3,0:T(8,128)}) fusion(f32[2,2,1024,1024]{2,3,1,0:T(8,128)S(1)} %bitcast.139, f32[2,2,1024]{2,1,0:T(2,128)S(1)} %log_add_fusion, bf16[1024,2,64,1]{0,2,3,1:T(8,128)(2,1)} %bitcast.153, bf16[1024,2,2,64]{0,3,2,1:T(8,128)(2,1)S(1)} %bitcast.149), kind=kOutput, calls=%fused_computation.2 | convolution fusion | flops 549449728 | bytes 34373632 | tf_op jit(solution)/shard_map/tkgd,skd->kgts/dot_general | solution.py:257
  436.7 8.3 %fusion.2 = bf16[2,2,1024,1024]{2,3,1,0:T(8,128)(2,1)S(1)} fusion(f32[2,1024,1024,2]{2,1,3,0:T(8,128)} %get-tuple-element.140, f32[2,2,1024,1024]{2,3,1,0:T(8,128)S(1)} %bitcast.139, f32[2,2,1024]{2,1,0:T(2,128)S(1)} %get-tuple-element.139, f32[2,2,1024]{2,1,0:T(2,128)S(1)} %log_add_fusion), kind=kLoop, calls=%fused_computation.4 | loop fusion | flops 16777216 | bytes 41975808 | tf_op jit(solution)/shard_map/convert_element_type | solution.py:262
  492.9 7.6 %collective-permute-done.72 = bf16[128,768]{0,1:T(8,128)(2,1)} collective-permute-done((bf16[128,768]{0,1:T(8,128)(2,1)}, bf16[128,768]{0,1:T(8,128)(2,1)}, u32[]{:S(2)}, u32[]{:S(2)}) %collective-permute-start.72) | collective-permute-done | bytes 196640 | tf_op jit(solution)/shard_map/ppermute | solution.py:51
  512.8 8.9 %collective-permute-done.76 = bf16[32,768]{0,1:T(8,128)(2,1)S(1)} collective-permute-done((bf16[32,768]{0,1:T(8,128)(2,1)S(1)}, bf16[32,768]{0,1:T(8,128)(2,1)S(1)}, u32[]{:S(2)}, u32[]{:S(2)}) %collective-permute-start.76) | collective-permute-done | bytes 49184 | tf_op jit(solution)/shard_map/ppermute | solution.py:19
  (552 shorter events, 280.0 us)
Async XLA Ops:
  0.7 56.2 %collective-permute-start.13 = (s32[1,256]{1,0:T(1,128)}, s32[1,256]{1,0:T(1,128)S(1)}, u32[]{:S(2)}, u32[]{:S(2)}) collective-permute-start(s32[1,256]{1,0:T(1,128)} %param.13), channel_id=1, source_target_pairs={{0,1},{1,0},{2,3},{3,2},{4,5},{5,4},{6,7},{7,6},{8,9},{9,8},{10,11... | collective-permute-start | bytes 3080 | tf_op jit(solution)/shard_map/ppermute | solution.py:19
  1.2 55.3 %collective-permute-start.14 = (s32[1,256]{1,0:T(1,128)}, s32[1,256]{1,0:T(1,128)S(1)}, u32[]{:S(2)}, u32[]{:S(2)}) collective-permute-start(s32[1,256]{1,0:T(1,128)} %param.13), channel_id=1, source_target_pairs={{0,2},{1,3},{2,0},{3,1},{4,6},{5,7},{6,4},{7,5},{8,10},{9,11},{10,... | collective-permute-start | bytes 3080 | tf_op jit(solution)/shard_map/ppermute | solution.py:19
  3.7 141.6 %collective-permute-start.1 = (bf16[256,1024]{1,0:T(8,128)(2,1)}, bf16[256,1024]{1,0:T(8,128)(2,1)S(1)}, u32[]{:S(2)}, u32[]{:S(2)}) collective-permute-start(bf16[256,1024]{1,0:T(8,128)(2,1)} %bitcast.143), channel_id=1, source_target_pairs={{0,2},{1,3},{2,0},{3,1},{4,6},{5,7},{6,4},{7,5},{8,10},{9,11},{10,... | collective-permute-start | bytes 1572872 | tf_op jit(solution)/shard_map/ppermute | solution.py:19
  3.8 164.2 %collective-permute-start = (bf16[256,1024]{1,0:T(8,128)(2,1)}, bf16[256,1024]{1,0:T(8,128)(2,1)S(1)}, u32[]{:S(2)}, u32[]{:S(2)}) collective-permute-start(bf16[256,1024]{1,0:T(8,128)(2,1)} %bitcast.144), channel_id=1, source_target_pairs={{0,1},{1,0},{2,3},{3,2},{4,5},{5,4},{6,7},{7,6},{8,9},{9,8},{10,11... | collective-permute-start | bytes 1572872 | tf_op jit(solution)/shard_map/ppermute | solution.py:19
  7.6 56.2 %collective-permute-start.4 = (bf16[32,768]{1,0:T(8,128)(2,1)}, bf16[32,768]{1,0:T(8,128)(2,1)S(1)}, u32[]{:S(2)}, u32[]{:S(2)}) collective-permute-start(bf16[32,768]{1,0:T(8,128)(2,1)} %pad_maximum_fusion.13), channel_id=1, source_target_pairs={{0,2},{1,3},{2,0},{3,1},{4,6},{5,7},{6,4},{7,5},{8,10},{9,11},{10,... | collective-permute-start | bytes 147464 | tf_op jit(solution)/shard_map/ppermute | solution.py:19
  91.0 23.3 %collective-permute-start.26 = (bf16[128,1152]{1,0:T(8,128)(2,1)S(1)}, bf16[128,1152]{1,0:T(8,128)(2,1)S(1)}, u32[]{:S(2)}, u32[]{:S(2)}) collective-permute-start(bf16[128,1152]{1,0:T(8,128)(2,1)S(1)} %constant_dynamic-update-slice_fusion.55), channel_id=1, source_target_pairs={{0,8},{4,12},{8,16},{12,20},{16,24},{20,28},{24,0},{28,4},{1,9},{5... | collective-permute-start | bytes 884744 | tf_op jit(solution)/shard_map/ppermute | solution.py:51
  130.3 26.8 %collective-permute-start.56 = (bf16[256,1024]{1,0:T(8,128)(2,1)}, bf16[256,1024]{1,0:T(8,128)(2,1)}, u32[]{:S(2)}, u32[]{:S(2)}) collective-permute-start(bf16[256,1024]{1,0:T(8,128)(2,1)} %bitcast.31), channel_id=1, source_target_pairs={{0,2},{1,3},{2,0},{3,1},{4,6},{5,7},{6,4},{7,5},{8,10},{9,11},{10,... | collective-permute-start | bytes 1572872 | tf_op jit(solution)/shard_map/ppermute | solution.py:19
  157.1 107.2 %collective-permute-start.55 = (bf16[256,1024]{1,0:T(8,128)(2,1)}, bf16[256,1024]{1,0:T(8,128)(2,1)}, u32[]{:S(2)}, u32[]{:S(2)}) collective-permute-start(bf16[256,1024]{1,0:T(8,128)(2,1)} %bitcast.31), channel_id=1, source_target_pairs={{0,1},{1,0},{2,3},{3,2},{4,5},{5,4},{6,7},{7,6},{8,9},{9,8},{10,11... | collective-permute-start | bytes 1572872 | tf_op jit(solution)/shard_map/ppermute | solution.py:19
  161.0 103.3 %collective-permute-start.57 = (bf16[256,1024]{1,0:T(8,128)(2,1)}, bf16[256,1024]{1,0:T(8,128)(2,1)}, u32[]{:S(2)}, u32[]{:S(2)}) collective-permute-start(bf16[256,1024]{1,0:T(8,128)(2,1)} %collective-permute-done.56), channel_id=1, source_target_pairs={{0,1},{1,0},{2,3},{3,2},{4,5},{5,4},{6,7},{7,6},{8,9},{9,8},{10,11... | collective-permute-start | bytes 1572872 | tf_op jit(solution)/shard_map/ppermute | solution.py:19
  167.0 39.4 %collective-permute-start.29 = (bf16[128,1152]{1,0:T(8,128)(2,1)}, bf16[128,1152]{1,0:T(8,128)(2,1)}, u32[]{:S(2)}, u32[]{:S(2)}) collective-permute-start(bf16[128,1152]{1,0:T(8,128)(2,1)} %collective-permute-done.28), channel_id=1, source_target_pairs={{0,4},{4,0},{8,12},{12,8},{16,20},{20,16},{24,28},{28,24},{1,5},{5... | collective-permute-start | bytes 884744 | tf_op jit(solution)/shard_map/ppermute | solution.py:19
  168.0 37.4 %collective-permute-start.49 = (bf16[128,1152]{1,0:T(8,128)(2,1)}, bf16[128,1152]{1,0:T(8,128)(2,1)}, u32[]{:S(2)}, u32[]{:S(2)}) collective-permute-start(bf16[128,1152]{1,0:T(8,128)(2,1)} %collective-permute-done.48), channel_id=1, source_target_pairs={{0,4},{4,0},{8,12},{12,8},{16,20},{20,16},{24,28},{28,24},{1,5},{5... | collective-permute-start | bytes 884744 | tf_op jit(solution)/shard_map/ppermute | solution.py:19
  169.8 33.6 %collective-permute-start.40 = (bf16[128,1152]{1,0:T(8,128)(2,1)}, bf16[128,1152]{1,0:T(8,128)(2,1)}, u32[]{:S(2)}, u32[]{:S(2)}) collective-permute-start(bf16[128,1152]{1,0:T(8,128)(2,1)} %collective-permute-done.38), channel_id=1, source_target_pairs={{0,8},{4,12},{8,16},{12,20},{16,24},{20,28},{24,0},{28,4},{1,9},{5... | collective-permute-start | bytes 884744 | tf_op jit(solution)/shard_map/ppermute | solution.py:51
  206.4 23.9 %collective-permute-start.50 = (bf16[128,1152]{1,0:T(8,128)(2,1)}, bf16[128,1152]{1,0:T(8,128)(2,1)S(1)}, u32[]{:S(2)}, u32[]{:S(2)}) collective-permute-start(bf16[128,1152]{1,0:T(8,128)(2,1)} %collective-permute-done.48), channel_id=1, source_target_pairs={{0,8},{4,12},{8,16},{12,20},{16,24},{20,28},{24,0},{28,4},{1,9},{5... | collective-permute-start | bytes 884744 | tf_op jit(solution)/shard_map/ppermute | solution.py:51
  230.3 22.4 %collective-permute-start.31 = (bf16[128,1152]{1,0:T(8,128)(2,1)S(1)}, bf16[128,1152]{1,0:T(8,128)(2,1)S(1)}, u32[]{:S(2)}, u32[]{:S(2)}) collective-permute-start(bf16[128,1152]{1,0:T(8,128)(2,1)S(1)} %collective-permute-done.30), channel_id=1, source_target_pairs={{0,4},{4,0},{8,12},{12,8},{16,20},{20,16},{24,28},{28,24},{1,5},{5... | collective-permute-start | bytes 884744 | tf_op jit(solution)/shard_map/ppermute | solution.py:19
  230.7 22.0 %collective-permute-start.51 = (bf16[128,1152]{1,0:T(8,128)(2,1)S(1)}, bf16[128,1152]{1,0:T(8,128)(2,1)S(1)}, u32[]{:S(2)}, u32[]{:S(2)}) collective-permute-start(bf16[128,1152]{1,0:T(8,128)(2,1)S(1)} %collective-permute-done.50), channel_id=1, source_target_pairs={{0,4},{4,0},{8,12},{12,8},{16,20},{20,16},{24,28},{28,24},{1,5},{5... | collective-permute-start | bytes 884744 | tf_op jit(solution)/shard_map/ppermute | solution.py:19
  284.7 102.2 %collective-permute-start.52 = (bf16[256,1024]{1,0:T(8,128)(2,1)S(1)}, bf16[256,1024]{1,0:T(8,128)(2,1)S(1)}, u32[]{:S(2)}, u32[]{:S(2)}) collective-permute-start(bf16[256,1024]{1,0:T(8,128)(2,1)S(1)} %get-tuple-element.46), channel_id=1, source_target_pairs={{0,1},{1,0},{2,3},{3,2},{4,5},{5,4},{6,7},{7,6},{8,9},{9,8},{10,11... | collective-permute-start | bytes 1572872 | tf_op jit(solution)/shard_map/ppermute | solution.py:19
  285.3 41.7 %collective-permute-start.53 = (bf16[256,1024]{1,0:T(8,128)(2,1)S(1)}, bf16[256,1024]{1,0:T(8,128)(2,1)S(1)}, u32[]{:S(2)}, u32[]{:S(2)}) collective-permute-start(bf16[256,1024]{1,0:T(8,128)(2,1)S(1)} %get-tuple-element.47), channel_id=1, source_target_pairs={{0,1},{1,0},{2,3},{3,2},{4,5},{5,4},{6,7},{7,6},{8,9},{9,8},{10,11... | collective-permute-start | bytes 1572872 | tf_op jit(solution)/shard_map/ppermute | solution.py:19
  290.3 38.9 %collective-permute-start.99 = (bf16[128,1152]{1,0:T(8,128)(2,1)S(1)}, bf16[128,1152]{1,0:T(8,128)(2,1)S(1)}, u32[]{:S(2)}, u32[]{:S(2)}) collective-permute-start(bf16[128,1152]{1,0:T(8,128)(2,1)S(1)} %get-tuple-element.32), channel_id=1, source_target_pairs={{0,4},{4,0},{8,12},{12,8},{16,20},{20,16},{24,28},{28,24},{1,5},{5... | collective-permute-start | bytes 884744 | tf_op jit(solution)/shard_map/ppermute | solution.py:19
  292.1 66.3 %collective-permute-start.98 = (bf16[128,1152]{1,0:T(8,128)(2,1)S(1)}, bf16[128,1152]{1,0:T(8,128)(2,1)S(1)}, u32[]{:S(2)}, u32[]{:S(2)}) collective-permute-start(bf16[128,1152]{1,0:T(8,128)(2,1)S(1)} %get-tuple-element.33), channel_id=1, source_target_pairs={{0,4},{4,0},{8,12},{12,8},{16,20},{20,16},{24,28},{28,24},{1,5},{5... | collective-permute-start | bytes 884744 | tf_op jit(solution)/shard_map/ppermute | solution.py:19
  328.8 55.5 %collective-permute-start.58 = (bf16[256,1024]{1,0:T(8,128)(2,1)S(1)}, bf16[256,1024]{1,0:T(8,128)(2,1)S(1)}, u32[]{:S(2)}, u32[]{:S(2)}) collective-permute-start(bf16[256,1024]{1,0:T(8,128)(2,1)S(1)} %get-tuple-element.44), channel_id=1, source_target_pairs={{0,1},{1,0},{2,3},{3,2},{4,5},{5,4},{6,7},{7,6},{8,9},{9,8},{10,11... | collective-permute-start | bytes 1572872 | tf_op jit(solution)/shard_map/ppermute | solution.py:19
  415.0 58.1 %collective-permute-start.86 = (bf16[32,1152]{1,0:T(8,128)(2,1)S(1)}, bf16[32,1152]{1,0:T(8,128)(2,1)S(1)}, u32[]{:S(2)}, u32[]{:S(2)}) collective-permute-start(bf16[32,1152]{1,0:T(8,128)(2,1)S(1)} %get-tuple-element.71), channel_id=1, source_target_pairs={{0,3},{1,2},{2,1},{3,0},{4,7},{5,6},{6,5},{7,4},{8,11},{9,10},{10,... | collective-permute-start | bytes 221192 | tf_op jit(solution)/shard_map/ppermute | solution.py:19
  473.7 31.1 %collective-permute-start.67 = (bf16[128,768]{0,1:T(8,128)(2,1)}, bf16[128,768]{0,1:T(8,128)(2,1)S(1)}, u32[]{:S(2)}, u32[]{:S(2)}) collective-permute-start(bf16[128,768]{0,1:T(8,128)(2,1)} %get-tuple-element.50), channel_id=1, source_target_pairs={{0,4},{4,0},{8,12},{12,8},{16,20},{20,16},{24,28},{28,24},{1,5},{5... | collective-permute-start | bytes 589832 | tf_op jit(solution)/shard_map/ppermute | solution.py:19
  482.7 44.6 %collective-permute-start.64 = (bf16[256,1024]{1,0:T(8,128)(2,1)}, bf16[256,1024]{1,0:T(8,128)(2,1)}, u32[]{:S(2)}, u32[]{:S(2)}) collective-permute-start(bf16[256,1024]{1,0:T(8,128)(2,1)} %get-tuple-element.42), channel_id=1, source_target_pairs={{0,1},{1,0},{2,3},{3,2},{4,5},{5,4},{6,7},{7,6},{8,9},{9,8},{10,11... | collective-permute-start | bytes 1572872 | tf_op jit(solution)/shard_map/ppermute | solution.py:19
  503.7 23.6 %collective-permute-start.66 = (bf16[256,1024]{1,0:T(8,128)(2,1)}, bf16[256,1024]{1,0:T(8,128)(2,1)}, u32[]{:S(2)}, u32[]{:S(2)}) collective-permute-start(bf16[256,1024]{1,0:T(8,128)(2,1)} %add_convert_fusion.1), channel_id=1, source_target_pairs={{0,2},{1,3},{2,0},{3,1},{4,6},{5,7},{6,4},{7,5},{8,10},{9,11},{10,... | collective-permute-start | bytes 1572872 | tf_op jit(solution)/shard_map/ppermute | solution.py:19
  (146 other events, 1807.2 us)
where the time goes:
time: 540 us; the launch traced here: 532 us
  waiting for transfers between devices  244 us (45%)
  matrix products  85.8 us (16%)
  starting transfers between devices  66.8 us (12%)
  other arithmetic  47.9 us (9%)
  local copies, waits for them, and re-layouts  42.3 us (8%)
  blocking collectives  41.8 us (8%)
    ppermute x24, waiting for transfers between devices, ring(): return lax.ppermute(value, 'dp', [(i, (i + 2) % size) for i in range(size)])  123 us
    ppermute x88, waiting for transfers between devices, flip(): return lax.ppermute(value, axis, [(i, i ^ bits) for i in range(size)])  121 us
    ppermute x88, starting transfers between devices, flip(): return lax.ppermute(value, axis, [(i, i ^ bits) for i in range(size)])  51.6 us
    all_gather x1, blocking collectives, on_device(): gains_full = lax.all_gather(norm_gains, ALL, axis=1, tiled=True).astype(F32)  41.8 us
    dot_general x7, matrix products, dot(): lax.dot_general(a, b, (((1,), (0,)), ((), ())), preferred_element_type=F32)  20.4 us
    dynamic_update_slice x68, local copies, waits for them, and re-layouts, place(): out = lax.dynamic_update_slice_in_dim(out, part, at * size, axis)  17.8 us
    dot_general x5, matrix products, dot_nt(): lax.dot_general(a, b, (((1,), (1,)), ((), ())), preferred_element_type=F32)  15.9 us
    ppermute x24, starting transfers between devices, ring(): return lax.ppermute(value, 'dp', [(i, (i + 2) % size) for i in range(size)])  15.2 us
  transfers between devices with their start and end apart: 112, of which 50 were waited for; matrix products, arithmetic and copies ran while one was open for 28% of the time, Pallas kernels for 0%

commit v1 on v0

--- a/solution.py
+++ b/solution.py
@@ -9,6 +9,26 @@
 BF = jnp.bfloat16
 F32 = jnp.float32
 ALL = ("dp", "ctx")
+
+
+def manage_floor_by_axis(obj, out_dim):
+    spare = list(obj.shape[1:])
+    spare[out_dim] *= obj.shape[0]
+    return jnp.moveaxis(obj, 0, out_dim).reshape(spare)
+
+
+def finish_scenes(local_block, along_axis):
+    piece_out = jax.lax.axis_index(along_axis)
+    heard = jax.lax.axis_size(along_axis)
+    vec_out, view_out = (heard, piece_out)
+    r1, latest = (local_block[None], 1)
+    while latest < vec_out:
+        answer = tuple(((ii, ii ^ latest) for ii in range(vec_out)))
+        finding = jax.lax.ppermute(r1, axis_name=along_axis, perm=answer)
+        part_next = view_out & latest == 0
+        r1 = jnp.concatenate([jnp.where(part_next, r1, finding), jnp.where(part_next, finding, r1)])
+        latest *= 2
+    return r1
 
 
 def add_low(a, b):
@@ -174,7 +194,11 @@
         block = place(exchange_ctx(sent), places, 0)
         return gather_dp(block, dp_size)
 
-    gains_full = lax.all_gather(norm_gains, ALL, axis=1, tiled=True).astype(F32)
+    def play_the_turns(arr_in, mine_x, dim_at):
+        a_now = finish_scenes(arr_in, mine_x)
+        return manage_floor_by_axis(a_now, dim_at)
+
+    gains_full = play_the_turns(norm_gains, ALL, 1).astype(F32)
     attn_w = spread([w_query, key_weight, value_weight, w_output.T])
     wq = attn_w[:, :q_cols]
     wk = attn_w[:, q_cols : q_cols + kv_cols]

time: 540 us -> 515 us (0.954)
  blocking collectives: 41.8 us -> 0 us
  starting transfers between devices: 66.8 us -> 99.8 us
  waiting for transfers between devices: 244 us -> 226 us
    all_gather x1 -> x0, blocking collectives: 41.8 us -> none  [on_device(): gains_full = lax.all_gather(norm_gains, ALL, axis=1, tiled=True).astype(F32)]
    ppermute x88, starting transfers between devices: 51.6 us -> 72.7 us  [flip(): return lax.ppermute(value, axis, [(i, i ^ bits) for i in range(size)])]
    ppermute x24, waiting for transfers between devices: 123 us -> 107 us  [ring(): return lax.ppermute(value, 'dp', [(i, (i + 2) % size) for i in range(size)])]
    ppermute x88, waiting for transfers between devices: 121 us -> 112 us  [flip(): return lax.ppermute(value, axis, [(i, i ^ bits) for i in range(size)])]
    ppermute x0 -> x5, starting transfers between devices: none -> 8.23 us  [finish_scenes(): finding = jax.lax.ppermute(r1, axis_name=along_axis, perm=answer)]
    ppermute x0 -> x5, waiting for transfers between devices: none -> 7.01 us  [finish_scenes(): finding = jax.lax.ppermute(r1, axis_name=along_axis, perm=answer)]
  transfers between devices with their start and end apart: 112 -> 117, of which waited for: 50 -> 53; matrix products, arithmetic and copies ran while one was open for 28% -> 29% of each run, Pallas kernels for 0% -> 0%
where the time goes in v1:
time: 515 us; the launch traced here: 507 us
  waiting for transfers between devices  226 us (44%)
  starting transfers between devices  99.8 us (19%)
  matrix products  85.8 us (17%)
  other arithmetic  47.4 us (9%)
  local copies, waits for them, and re-layouts  44.8 us (9%)
    ppermute x88, waiting for transfers between devices, flip(): return lax.ppermute(value, axis, [(i, i ^ bits) for i in range(size)])  112 us
    ppermute x24, waiting for transfers between devices, ring(): return lax.ppermute(value, 'dp', [(i, (i + 2) % size) for i in range(size)])  107 us
    ppermute x88, starting transfers between devices, flip(): return lax.ppermute(value, axis, [(i, i ^ bits) for i in range(size)])  72.7 us
    dot_general x7, matrix products, dot(): lax.dot_general(a, b, (((1,), (0,)), ((), ())), preferred_element_type=F32)  20.3 us
    dynamic_update_slice x68, local copies, waits for them, and re-layouts, place(): out = lax.dynamic_update_slice_in_dim(out, part, at * size, axis)  20.2 us
    ppermute x24, starting transfers between devices, ring(): return lax.ppermute(value, 'dp', [(i, (i + 2) % size) for i in range(size)])  18.9 us
    dot_general x5, matrix products, dot_nt(): lax.dot_general(a, b, (((1,), (1,)), ((), ())), preferred_element_type=F32)  15.9 us
    dot_general x5, matrix products, dot_tn(): lax.dot_general(a, b, (((0,), (0,)), ((), ())), preferred_element_type=F32)  14.5 us
  transfers between devices with their start and end apart: 117, of which 53 were waited for; matrix products, arithmetic and copies ran while one was open for 29% of the time, Pallas kernels for 0%

profile of v1, /device:TPU:0, one launch (start us, length us, event | category | flops | bytes accessed | tf_op | source)
XLA Modules:
  0.0 506.8 jit_solution(18053623180446528727)
XLA Ops:
  71.9 7.2 %collective-permute-done.41 = bf16[128,1152]{1,0:T(8,128)(2,1)S(1)} collective-permute-done((bf16[128,1152]{1,0:T(8,128)(2,1)S(1)}, bf16[128,1152]{1,0:T(8,128)(2,1)S(1)}, u32[]{:S(2)}, u32[]{:S(2)}) %collective-permute-start.41) | collective-permute-done | bytes 294944 | tf_op jit(solution)/shard_map/ppermute | solution.py:71
  90.2 6.6 %collective-permute-done.14 = bf16[128,768]{1,0:T(8,128)(2,1)S(1)} collective-permute-done((bf16[128,768]{1,0:T(8,128)(2,1)S(1)}, bf16[128,768]{1,0:T(8,128)(2,1)S(1)}, u32[]{:S(2)}, u32[]{:S(2)}) %collective-permute-start.14) | collective-permute-done | bytes 196640 | tf_op jit(solution)/shard_map/ppermute | solution.py:71
  108.7 9.4 %collective-permute-done.43 = bf16[128,1152]{1,0:T(8,128)(2,1)} collective-permute-done((bf16[128,1152]{1,0:T(8,128)(2,1)S(1)}, bf16[128,1152]{1,0:T(8,128)(2,1)}, u32[]{:S(2)}, u32[]{:S(2)}) %collective-permute-start.43) | collective-permute-done | bytes 294944 | tf_op jit(solution)/shard_map/ppermute | solution.py:71
  153.9 7.4 %fusion.96 = (f32[2,2,1024]{2,1,0:T(2,128)S(1)}, f32[2,2,1024,1024]{2,3,1,0:T(8,128)}) fusion(bf16[1024,2,64,1]{0,2,3,1:T(8,128)(2,1)S(1)} %fusion.47, bf16[1024,2,2,64]{0,3,2,1:T(8,128)(2,1)S(1)} %fusion.34, pred[1024,1024]{0,1:T(8,128)(4,1)S(1)} %copy-done.26), kind=kOutput, calls=%fused_computation.362 | convolution fusion | flops 549449728 | bytes 18628608 | tf_op jit(solution)/shard_map/tkgd,skd->kgts/dot_general | solution.py:232
  161.4 8.0 %fusion.3 = f32[2,2,1024]{2,1,0:T(2,128)S(1)} fusion(f32[2,2,1024,1024]{2,3,1,0:T(8,128)} %get-tuple-element.148, f32[2,2,1024]{2,1,0:T(2,128)S(1)} %get-tuple-element.147), kind=kLoop, calls=%fused_computation.9 | loop fusion | flops 8384512 | bytes 16809984 | tf_op jit(solution)/shard_map/reduce_sum | solution.py:238
  169.4 7.5 %fusion.18 = bf16[2,64,2,1024]{3,1,2,0:T(8,128)(2,1)S(1)} fusion(bf16[1024,2,64,1]{0,2,3,1:T(8,128)(2,1)S(1)} %bitcast.149, f32[2,2,1024,1024]{2,3,1,0:T(8,128)} %get-tuple-element.148, f32[2,2,1024]{2,1,0:T(2,128)S(1)} %fusion.3, f32[2,2,1024]{2,1,0:T(2,128)S(1)} %get-tuple-element.147), kind=kOutput, calls=%fused_computation.68 | convolution fusion | flops 549715968 | bytes 17596416 | tf_op jit(solution)/shard_map/kgts,skd->tkgd/dot_general | solution.py:241
  180.9 13.0 %collective-permute-start.55 = (bf16[128,1152]{1,0:T(8,128)(2,1)}, bf16[128,1152]{1,0:T(8,128)(2,1)S(1)}, u32[]{:S(2)}, u32[]{:S(2)}) collective-permute-start(bf16[128,1152]{1,0:T(8,128)(2,1)} %collective-permute-done.53), channel_id=1, source_target_pairs={{0,8},{4,12},{8,16},{12,20},{16,24},{20,28},{24,0},{28,4},{1,9},{5... | collective-permute-start | bytes 884744 | tf_op jit(solution)/shard_map/ppermute | solution.py:71
  196.3 8.4 %collective-permute-done.55 = bf16[128,1152]{1,0:T(8,128)(2,1)S(1)} collective-permute-done((bf16[128,1152]{1,0:T(8,128)(2,1)}, bf16[128,1152]{1,0:T(8,128)(2,1)S(1)}, u32[]{:S(2)}, u32[]{:S(2)}) %collective-permute-start.55) | collective-permute-done | bytes 294944 | tf_op jit(solution)/shard_map/ppermute | solution.py:71
  211.7 14.4 %collective-permute-done.46 = bf16[128,1152]{1,0:T(8,128)(2,1)S(1)} collective-permute-done((bf16[128,1152]{1,0:T(8,128)(2,1)}, bf16[128,1152]{1,0:T(8,128)(2,1)S(1)}, u32[]{:S(2)}, u32[]{:S(2)}) %collective-permute-start.46) | collective-permute-done | bytes 294944 | tf_op jit(solution)/shard_map/ppermute | solution.py:39
  228.0 10.7 %collective-permute-done.25 = bf16[256,1024]{1,0:T(8,128)(2,1)S(1)} collective-permute-done((bf16[256,1024]{1,0:T(8,128)(2,1)S(1)}, bf16[256,1024]{1,0:T(8,128)(2,1)S(1)}, u32[]{:S(2)}, u32[]{:S(2)}) %collective-permute-start.25) | collective-permute-done | bytes 524320 | tf_op jit(solution)/shard_map/ppermute | solution.py:39
  247.7 8.2 %fusion.13 = (bf16[1024,1152]{1,0:T(8,128)(2,1)}, bf16[1024,1152]{1,0:T(8,128)(2,1)}, bf16[1024,1152]{1,0:T(8,128)(2,1)S(1)}) fusion(f32[1024,1152]{1,0:T(8,128)S(1)} %fusion.46, f32[1024,1152]{1,0:T(8,128)S(1)} %fusion.77, bf16[1024,1152]{1,0:T(8,128)(2,1)S(1)} %constant_dynamic-update-slice_fusion.47, bf16[256,1024]{1,0:T(8,128)(2,1)S(1)} %collective-permute-done.26, ...), kind=kOutput, calls=%fused_computation.21 | convolution fusion | flops 2443182080 | bytes 20971520 | tf_op jit(solution)/shard_map/dot_general | solution.py:119
  284.8 8.0 %collective-permute-done.95 = bf16[128,1152]{1,0:T(8,128)(2,1)S(1)} collective-permute-done((bf16[128,1152]{1,0:T(8,128)(2,1)S(1)}, bf16[128,1152]{1,0:T(8,128)(2,1)S(1)}, u32[]{:S(2)}, u32[]{:S(2)}) %collective-permute-start.95) | collective-permute-done | bytes 294944 | tf_op jit(solution)/shard_map/ppermute | solution.py:39
  294.4 6.8 %collective-permute-done.85 = bf16[128,1152]{1,0:T(8,128)(2,1)S(1)} collective-permute-done((bf16[128,1152]{1,0:T(8,128)(2,1)S(1)}, bf16[128,1152]{1,0:T(8,128)(2,1)S(1)}, u32[]{:S(2)}, u32[]{:S(2)}) %collective-permute-start.85) | collective-permute-done | bytes 294944 | tf_op jit(solution)/shard_map/ppermute | solution.py:39
  305.2 7.3 %collective-permute-done.106 = bf16[128,1152]{1,0:T(8,128)(2,1)S(1)} collective-permute-done((bf16[128,1152]{1,0:T(8,128)(2,1)S(1)}, bf16[128,1152]{1,0:T(8,128)(2,1)S(1)}, u32[]{:S(2)}, u32[]{:S(2)}) %collective-permute-start.106) | collective-permute-done | bytes 294944 | tf_op jit(solution)/shard_map/ppermute | solution.py:71
  314.5 8.4 %collective-permute-done.96 = bf16[128,1152]{1,0:T(8,128)(2,1)S(1)} collective-permute-done((bf16[128,1152]{1,0:T(8,128)(2,1)S(1)}, bf16[128,1152]{1,0:T(8,128)(2,1)S(1)}, u32[]{:S(2)}, u32[]{:S(2)}) %collective-permute-start.96) | collective-permute-done | bytes 294944 | tf_op jit(solution)/shard_map/ppermute | solution.py:71
  324.9 7.6 %collective-permute-done.86 = bf16[128,1152]{1,0:T(8,128)(2,1)S(1)} collective-permute-done((bf16[128,1152]{1,0:T(8,128)(2,1)S(1)}, bf16[128,1152]{1,0:T(8,128)(2,1)S(1)}, u32[]{:S(2)}, u32[]{:S(2)}) %collective-permute-start.86) | collective-permute-done | bytes 294944 | tf_op jit(solution)/shard_map/ppermute | solution.py:71
  334.4 6.7 %collective-permute-done.107 = bf16[128,1152]{1,0:T(8,128)(2,1)S(1)} collective-permute-done((bf16[128,1152]{1,0:T(8,128)(2,1)S(1)}, bf16[128,1152]{1,0:T(8,128)(2,1)S(1)}, u32[]{:S(2)}, u32[]{:S(2)}) %collective-permute-start.107) | collective-permute-done | bytes 294944 | tf_op jit(solution)/shard_map/ppermute | solution.py:71
  342.3 7.3 %collective-permute-done.97 = bf16[128,1152]{1,0:T(8,128)(2,1)S(1)} collective-permute-done((bf16[128,1152]{1,0:T(8,128)(2,1)S(1)}, bf16[128,1152]{1,0:T(8,128)(2,1)S(1)}, u32[]{:S(2)}, u32[]{:S(2)}) %collective-permute-start.97) | collective-permute-done | bytes 294944 | tf_op jit(solution)/shard_map/ppermute | solution.py:71
  351.5 6.6 %collective-permute-done.87 = bf16[128,1152]{1,0:T(8,128)(2,1)S(1)} collective-permute-done((bf16[128,1152]{1,0:T(8,128)(2,1)S(1)}, bf16[128,1152]{1,0:T(8,128)(2,1)S(1)}, u32[]{:S(2)}, u32[]{:S(2)}) %collective-permute-start.87) | collective-permute-done | bytes 294944 | tf_op jit(solution)/shard_map/ppermute | solution.py:71
  361.9 6.6 %collective-permute-done.59 = bf16[256,1024]{1,0:T(8,128)(2,1)S(1)} collective-permute-done((bf16[256,1024]{1,0:T(8,128)(2,1)S(1)}, bf16[256,1024]{1,0:T(8,128)(2,1)S(1)}, u32[]{:S(2)}, u32[]{:S(2)}) %collective-permute-start.59) | collective-permute-done | bytes 524320 | tf_op jit(solution)/shard_map/ppermute | solution.py:39
  401.9 8.5 %fusion = (f32[2,2,1024]{2,1,0:T(2,128)S(1)}, f32[2,1024,1024,2]{2,1,3,0:T(8,128)}) fusion(f32[2,2,1024,1024]{2,3,1,0:T(8,128)S(1)} %bitcast.136, f32[2,2,1024]{2,1,0:T(2,128)S(1)} %log_add_fusion, bf16[1024,2,64,1]{0,2,3,1:T(8,128)(2,1)} %bitcast.150, bf16[1024,2,2,64]{0,3,2,1:T(8,128)(2,1)S(1)} %bitcast.146), kind=kOutput, calls=%fused_computation.2 | convolution fusion | flops 549449728 | bytes 34373632 | tf_op jit(solution)/shard_map/tkgd,skd->kgts/dot_general | solution.py:281
  410.4 8.3 %fusion.2 = bf16[2,2,1024,1024]{2,3,1,0:T(8,128)(2,1)S(1)} fusion(f32[2,1024,1024,2]{2,1,3,0:T(8,128)} %get-tuple-element.150, f32[2,2,1024,1024]{2,3,1,0:T(8,128)S(1)} %bitcast.136, f32[2,2,1024]{2,1,0:T(2,128)S(1)} %get-tuple-element.149, f32[2,2,1024]{2,1,0:T(2,128)S(1)} %log_add_fusion), kind=kLoop, calls=%fused_computation.4 | loop fusion | flops 16777216 | bytes 41975808 | tf_op jit(solution)/shard_map/convert_element_type | solution.py:286
  467.7 7.6 %collective-permute-done.77 = bf16[128,768]{0,1:T(8,128)(2,1)} collective-permute-done((bf16[128,768]{0,1:T(8,128)(2,1)}, bf16[128,768]{0,1:T(8,128)(2,1)}, u32[]{:S(2)}, u32[]{:S(2)}) %collective-permute-start.77) | collective-permute-done | bytes 196640 | tf_op jit(solution)/shard_map/ppermute | solution.py:71
  487.6 8.8 %collective-permute-done.81 = bf16[32,768]{0,1:T(8,128)(2,1)S(1)} collective-permute-done((bf16[32,768]{0,1:T(8,128)(2,1)S(1)}, bf16[32,768]{0,1:T(8,128)(2,1)S(1)}, u32[]{:S(2)}, u32[]{:S(2)}) %collective-permute-start.81) | collective-permute-done | bytes 49184 | tf_op jit(solution)/shard_map/ppermute | solution.py:39
  (573 shorter events, 304.6 us)
Async XLA Ops:
  0.7 24.8 %collective-permute-start.18 = (s32[1,256]{1,0:T(1,128)}, s32[1,256]{1,0:T(1,128)S(1)}, u32[]{:S(2)}, u32[]{:S(2)}) collective-permute-start(s32[1,256]{1,0:T(1,128)} %param.13), channel_id=1, source_target_pairs={{0,1},{1,0},{2,3},{3,2},{4,5},{5,4},{6,7},{7,6},{8,9},{9,8},{10,11... | collective-permute-start | bytes 3080 | tf_op jit(solution)/shard_map/ppermute | solution.py:39
  1.2 22.2 %collective-permute-start.19 = (s32[1,256]{1,0:T(1,128)}, s32[1,256]{1,0:T(1,128)S(1)}, u32[]{:S(2)}, u32[]{:S(2)}) collective-permute-start(s32[1,256]{1,0:T(1,128)} %param.13), channel_id=1, source_target_pairs={{0,2},{1,3},{2,0},{3,1},{4,6},{5,7},{6,4},{7,5},{8,10},{9,11},{10,... | collective-permute-start | bytes 3080 | tf_op jit(solution)/shard_map/ppermute | solution.py:39
  3.8 117.6 %collective-permute-start.1 = (bf16[256,1024]{1,0:T(8,128)(2,1)}, bf16[256,1024]{1,0:T(8,128)(2,1)S(1)}, u32[]{:S(2)}, u32[]{:S(2)}) collective-permute-start(bf16[256,1024]{1,0:T(8,128)(2,1)} %bitcast.140), channel_id=1, source_target_pairs={{0,2},{1,3},{2,0},{3,1},{4,6},{5,7},{6,4},{7,5},{8,10},{9,11},{10,... | collective-permute-start | bytes 1572872 | tf_op jit(solution)/shard_map/ppermute | solution.py:39
  3.8 139.9 %collective-permute-start = (bf16[256,1024]{1,0:T(8,128)(2,1)}, bf16[256,1024]{1,0:T(8,128)(2,1)S(1)}, u32[]{:S(2)}, u32[]{:S(2)}) collective-permute-start(bf16[256,1024]{1,0:T(8,128)(2,1)} %bitcast.141), channel_id=1, source_target_pairs={{0,1},{1,0},{2,3},{3,2},{4,5},{5,4},{6,7},{7,6},{8,9},{9,8},{10,11... | collective-permute-start | bytes 1572872 | tf_op jit(solution)/shard_map/ppermute | solution.py:39
  64.7 24.8 %collective-permute-start.31 = (bf16[128,1152]{1,0:T(8,128)(2,1)S(1)}, bf16[128,1152]{1,0:T(8,128)(2,1)S(1)}, u32[]{:S(2)}, u32[]{:S(2)}) collective-permute-start(bf16[128,1152]{1,0:T(8,128)(2,1)S(1)} %constant_dynamic-update-slice_fusion.55), channel_id=1, source_target_pairs={{0,8},{4,12},{8,16},{12,20},{16,24},{20,28},{24,0},{28,4},{1,9},{5... | collective-permute-start | bytes 884744 | tf_op jit(solution)/shard_map/ppermute | solution.py:71
  104.6 27.8 %collective-permute-start.61 = (bf16[256,1024]{1,0:T(8,128)(2,1)}, bf16[256,1024]{1,0:T(8,128)(2,1)}, u32[]{:S(2)}, u32[]{:S(2)}) collective-permute-start(bf16[256,1024]{1,0:T(8,128)(2,1)} %bitcast.28), channel_id=1, source_target_pairs={{0,2},{1,3},{2,0},{3,1},{4,6},{5,7},{6,4},{7,5},{8,10},{9,11},{10,... | collective-permute-start | bytes 1572872 | tf_op jit(solution)/shard_map/ppermute | solution.py:39
  132.4 106.3 %collective-permute-start.60 = (bf16[256,1024]{1,0:T(8,128)(2,1)}, bf16[256,1024]{1,0:T(8,128)(2,1)}, u32[]{:S(2)}, u32[]{:S(2)}) collective-permute-start(bf16[256,1024]{1,0:T(8,128)(2,1)} %bitcast.28), channel_id=1, source_target_pairs={{0,1},{1,0},{2,3},{3,2},{4,5},{5,4},{6,7},{7,6},{8,9},{9,8},{10,11... | collective-permute-start | bytes 1572872 | tf_op jit(solution)/shard_map/ppermute | solution.py:39
  135.5 103.2 %collective-permute-start.62 = (bf16[256,1024]{1,0:T(8,128)(2,1)}, bf16[256,1024]{1,0:T(8,128)(2,1)}, u32[]{:S(2)}, u32[]{:S(2)}) collective-permute-start(bf16[256,1024]{1,0:T(8,128)(2,1)} %collective-permute-done.61), channel_id=1, source_target_pairs={{0,1},{1,0},{2,3},{3,2},{4,5},{5,4},{6,7},{7,6},{8,9},{9,8},{10,11... | collective-permute-start | bytes 1572872 | tf_op jit(solution)/shard_map/ppermute | solution.py:39
  141.4 39.5 %collective-permute-start.34 = (bf16[128,1152]{1,0:T(8,128)(2,1)}, bf16[128,1152]{1,0:T(8,128)(2,1)}, u32[]{:S(2)}, u32[]{:S(2)}) collective-permute-start(bf16[128,1152]{1,0:T(8,128)(2,1)} %collective-permute-done.33), channel_id=1, source_target_pairs={{0,4},{4,0},{8,12},{12,8},{16,20},{20,16},{24,28},{28,24},{1,5},{5... | collective-permute-start | bytes 884744 | tf_op jit(solution)/shard_map/ppermute | solution.py:39
  143.7 36.2 %collective-permute-start.54 = (bf16[128,1152]{1,0:T(8,128)(2,1)}, bf16[128,1152]{1,0:T(8,128)(2,1)}, u32[]{:S(2)}, u32[]{:S(2)}) collective-permute-start(bf16[128,1152]{1,0:T(8,128)(2,1)} %collective-permute-done.53), channel_id=1, source_target_pairs={{0,4},{4,0},{8,12},{12,8},{16,20},{20,16},{24,28},{28,24},{1,5},{5... | collective-permute-start | bytes 884744 | tf_op jit(solution)/shard_map/ppermute | solution.py:39
  144.2 33.6 %collective-permute-start.45 = (bf16[128,1152]{1,0:T(8,128)(2,1)}, bf16[128,1152]{1,0:T(8,128)(2,1)}, u32[]{:S(2)}, u32[]{:S(2)}) collective-permute-start(bf16[128,1152]{1,0:T(8,128)(2,1)} %collective-permute-done.43), channel_id=1, source_target_pairs={{0,8},{4,12},{8,16},{12,20},{16,24},{20,28},{24,0},{28,4},{1,9},{5... | collective-permute-start | bytes 884744 | tf_op jit(solution)/shard_map/ppermute | solution.py:71
  180.9 23.9 %collective-permute-start.55 = (bf16[128,1152]{1,0:T(8,128)(2,1)}, bf16[128,1152]{1,0:T(8,128)(2,1)S(1)}, u32[]{:S(2)}, u32[]{:S(2)}) collective-permute-start(bf16[128,1152]{1,0:T(8,128)(2,1)} %collective-permute-done.53), channel_id=1, source_target_pairs={{0,8},{4,12},{8,16},{12,20},{16,24},{20,28},{24,0},{28,4},{1,9},{5... | collective-permute-start | bytes 884744 | tf_op jit(solution)/shard_map/ppermute | solution.py:71
  204.8 23.1 %collective-permute-start.36 = (bf16[128,1152]{1,0:T(8,128)(2,1)S(1)}, bf16[128,1152]{1,0:T(8,128)(2,1)S(1)}, u32[]{:S(2)}, u32[]{:S(2)}) collective-permute-start(bf16[128,1152]{1,0:T(8,128)(2,1)S(1)} %collective-permute-done.35), channel_id=1, source_target_pairs={{0,4},{4,0},{8,12},{12,8},{16,20},{20,16},{24,28},{28,24},{1,5},{5... | collective-permute-start | bytes 884744 | tf_op jit(solution)/shard_map/ppermute | solution.py:39
  206.4 21.4 %collective-permute-start.56 = (bf16[128,1152]{1,0:T(8,128)(2,1)S(1)}, bf16[128,1152]{1,0:T(8,128)(2,1)S(1)}, u32[]{:S(2)}, u32[]{:S(2)}) collective-permute-start(bf16[128,1152]{1,0:T(8,128)(2,1)S(1)} %collective-permute-done.55), channel_id=1, source_target_pairs={{0,4},{4,0},{8,12},{12,8},{16,20},{20,16},{24,28},{28,24},{1,5},{5... | collective-permute-start | bytes 884744 | tf_op jit(solution)/shard_map/ppermute | solution.py:39
  259.1 102.7 %collective-permute-start.57 = (bf16[256,1024]{1,0:T(8,128)(2,1)S(1)}, bf16[256,1024]{1,0:T(8,128)(2,1)S(1)}, u32[]{:S(2)}, u32[]{:S(2)}) collective-permute-start(bf16[256,1024]{1,0:T(8,128)(2,1)S(1)} %get-tuple-element.48), channel_id=1, source_target_pairs={{0,1},{1,0},{2,3},{3,2},{4,5},{5,4},{6,7},{7,6},{8,9},{9,8},{10,11... | collective-permute-start | bytes 1572872 | tf_op jit(solution)/shard_map/ppermute | solution.py:39
  259.7 41.5 %collective-permute-start.58 = (bf16[256,1024]{1,0:T(8,128)(2,1)S(1)}, bf16[256,1024]{1,0:T(8,128)(2,1)S(1)}, u32[]{:S(2)}, u32[]{:S(2)}) collective-permute-start(bf16[256,1024]{1,0:T(8,128)(2,1)S(1)} %get-tuple-element.49), channel_id=1, source_target_pairs={{0,1},{1,0},{2,3},{3,2},{4,5},{5,4},{6,7},{7,6},{8,9},{9,8},{10,11... | collective-permute-start | bytes 1572872 | tf_op jit(solution)/shard_map/ppermute | solution.py:39
  266.0 37.4 %collective-permute-start.104 = (bf16[128,1152]{1,0:T(8,128)(2,1)S(1)}, bf16[128,1152]{1,0:T(8,128)(2,1)S(1)}, u32[]{:S(2)}, u32[]{:S(2)}) collective-permute-start(bf16[128,1152]{1,0:T(8,128)(2,1)S(1)} %get-tuple-element.34), channel_id=1, source_target_pairs={{0,4},{4,0},{8,12},{12,8},{16,20},{20,16},{24,28},{28,24},{1,5},{5... | collective-permute-start | bytes 884744 | tf_op jit(solution)/shard_map/ppermute | solution.py:39
  266.4 66.2 %collective-permute-start.103 = (bf16[128,1152]{1,0:T(8,128)(2,1)S(1)}, bf16[128,1152]{1,0:T(8,128)(2,1)S(1)}, u32[]{:S(2)}, u32[]{:S(2)}) collective-permute-start(bf16[128,1152]{1,0:T(8,128)(2,1)S(1)} %get-tuple-element.35), channel_id=1, source_target_pairs={{0,4},{4,0},{8,12},{12,8},{16,20},{20,16},{24,28},{28,24},{1,5},{5... | collective-permute-start | bytes 884744 | tf_op jit(solution)/shard_map/ppermute | solution.py:39
  303.0 56.2 %collective-permute-start.63 = (bf16[256,1024]{1,0:T(8,128)(2,1)S(1)}, bf16[256,1024]{1,0:T(8,128)(2,1)S(1)}, u32[]{:S(2)}, u32[]{:S(2)}) collective-permute-start(bf16[256,1024]{1,0:T(8,128)(2,1)S(1)} %get-tuple-element.46), channel_id=1, source_target_pairs={{0,1},{1,0},{2,3},{3,2},{4,5},{5,4},{6,7},{7,6},{8,9},{9,8},{10,11... | collective-permute-start | bytes 1572872 | tf_op jit(solution)/shard_map/ppermute | solution.py:39
  349.7 21.3 %collective-permute-start.102 = (bf16[128,1152]{1,0:T(8,128)(2,1)S(1)}, bf16[128,1152]{1,0:T(8,128)(2,1)S(1)}, u32[]{:S(2)}, u32[]{:S(2)}) collective-permute-start(bf16[128,1152]{1,0:T(8,128)(2,1)S(1)} %get-tuple-element.32), channel_id=1, source_target_pairs={{0,4},{4,0},{8,12},{12,8},{16,20},{20,16},{24,28},{28,24},{1,5},{5... | collective-permute-start | bytes 884744 | tf_op jit(solution)/shard_map/ppermute | solution.py:39
  388.5 58.2 %collective-permute-start.91 = (bf16[32,1152]{1,0:T(8,128)(2,1)S(1)}, bf16[32,1152]{1,0:T(8,128)(2,1)S(1)}, u32[]{:S(2)}, u32[]{:S(2)}) collective-permute-start(bf16[32,1152]{1,0:T(8,128)(2,1)S(1)} %get-tuple-element.73), channel_id=1, source_target_pairs={{0,3},{1,2},{2,1},{3,0},{4,7},{5,6},{6,5},{7,4},{8,11},{9,10},{10,... | collective-permute-start | bytes 221192 | tf_op jit(solution)/shard_map/ppermute | solution.py:39
  447.4 32.3 %collective-permute-start.72 = (bf16[128,768]{0,1:T(8,128)(2,1)}, bf16[128,768]{0,1:T(8,128)(2,1)S(1)}, u32[]{:S(2)}, u32[]{:S(2)}) collective-permute-start(bf16[128,768]{0,1:T(8,128)(2,1)} %get-tuple-element.52), channel_id=1, source_target_pairs={{0,4},{4,0},{8,12},{12,8},{16,20},{20,16},{24,28},{28,24},{1,5},{5... | collective-permute-start | bytes 589832 | tf_op jit(solution)/shard_map/ppermute | solution.py:39
  458.3 43.8 %collective-permute-start.69 = (bf16[256,1024]{1,0:T(8,128)(2,1)}, bf16[256,1024]{1,0:T(8,128)(2,1)}, u32[]{:S(2)}, u32[]{:S(2)}) collective-permute-start(bf16[256,1024]{1,0:T(8,128)(2,1)} %get-tuple-element.44), channel_id=1, source_target_pairs={{0,1},{1,0},{2,3},{3,2},{4,5},{5,4},{6,7},{7,6},{8,9},{9,8},{10,11... | collective-permute-start | bytes 1572872 | tf_op jit(solution)/shard_map/ppermute | solution.py:39
  478.6 23.6 %collective-permute-start.71 = (bf16[256,1024]{1,0:T(8,128)(2,1)}, bf16[256,1024]{1,0:T(8,128)(2,1)}, u32[]{:S(2)}, u32[]{:S(2)}) collective-permute-start(bf16[256,1024]{1,0:T(8,128)(2,1)} %add_convert_fusion.1), channel_id=1, source_target_pairs={{0,2},{1,3},{2,0},{3,1},{4,6},{5,7},{6,4},{7,5},{8,10},{9,11},{10,... | collective-permute-start | bytes 1572872 | tf_op jit(solution)/shard_map/ppermute | solution.py:39
  (152 other events, 1764.6 us)
